TPU v7x, 256 devices: a whole 4x4x8 slice. The times are simulated.
256 devices in a mesh: frame: 16 (over z_hi, y, core), row: 16 (over x, z_lo).
Axes of the slice: x: 4, y: 4, z: 8 (z_hi: 2, z_lo: 4; z = z_hi * 4 + z_lo), core: 2. Of those that a mesh axis runs over, the one named last changes fastest.
Arguments:
- latent: bfloat16 [64, 32, 240, 320], P('frame', 'row'), may hold values from -6 to 6
- gain_one: float32 [320], replicated, may hold values from 0.1 to 1.9
- spatial_weight: bfloat16 [3, 3, 320, 320], replicated, may hold values from -0.109375 to 0.109375
- gain_two: float32 [320], replicated, may hold values from 0.1 to 1.9
- temporal_weight: bfloat16 [3, 320, 320], replicated, may hold values from -0.1875 to 0.1875
- gain_three: float32 [320], replicated, may hold values from 0.1 to 1.9
- query_weight: bfloat16 [320, 320], replicated, as said below
- key_weight: bfloat16 [320, 320], replicated, may hold values from -0.3125 to 0.3125
- value_weight: bfloat16 [320, 320], replicated, may hold values from -0.3125 to 0.3125
- out_weight: bfloat16 [320, 320], replicated, may hold values from -0.3125 to 0.3125
Outputs:
- block_out: float32 [64, 32, 240, 320], P('frame', 'row')
Inputs may be any that keep to these rules, and one draw needn't show every extreme that they name: `query_weight`: a projection matrix.
All inputs are finite; a program needn't handle non-finite values.
Results may differ from a plain program's by a relative error of at most 0.012.
The roundings to bfloat16 on the way count: a program that leaves them out, or rounds other values in their place, can miss the bound.
Values may be sent and summed in bfloat16 or wider, within the bound.
A program may use at most 128 MiB of HBM per device.

v0:
```python
import jax
import jax.numpy as jnp
from jax import lax
from jax.sharding import PartitionSpec as P

HEAD_DIM = 64


def extended(cells, sides, width):
    for axis, dim in sides:
        count = lax.axis_size(axis)
        ends = count - 1
        head = lax.slice_in_dim(cells, 0, width, axis=dim)
        tail = lax.slice_in_dim(cells, cells.shape[dim] - width, cells.shape[dim], axis=dim)
        cells = jnp.concatenate(
            [
                lax.ppermute(tail, axis, [(i, (i + 1) % count) for i in range(ends)]),
                cells,
                lax.ppermute(head, axis, [((i + 1) % count, i) for i in range(ends)]),
            ],
            axis=dim,
        )
    return cells


def rms_norm(values, gain):
    mean_sq = jnp.mean(values * values, axis=-1, keepdims=True)
    return values * lax.rsqrt(mean_sq + 1e-06) * gain


def project(normed, weight):
    chans = normed.shape[-1]
    flat = jnp.dot(normed.reshape(-1, chans), weight, preferred_element_type=jnp.float32)
    return flat.astype(jnp.bfloat16).reshape(normed.shape[:-1] + (weight.shape[1],))


def attend_heads(queries, keys, values):
    frames, pixels, chans = queries.shape
    heads = chans // HEAD_DIM
    q_split = queries.reshape(frames, pixels, heads, HEAD_DIM)
    k_split = keys.reshape(frames, pixels, heads, HEAD_DIM)
    v_split = values.reshape(frames, pixels, heads, HEAD_DIM)
    scores = jnp.einsum(
        "fphd,gphd->phfg", q_split, k_split, preferred_element_type=jnp.float32
    ) / jnp.sqrt(jnp.float32(HEAD_DIM))
    peak = jnp.max(scores, axis=-1, keepdims=True)
    expo = jnp.exp(scores - peak)
    total = jnp.sum(expo, axis=-1)
    weight = expo.astype(jnp.bfloat16)
    summed = jnp.einsum("phfg,gphd->fphd", weight, v_split, preferred_element_type=jnp.float32)
    summed = summed / jnp.transpose(total, (2, 0, 1))[..., None]
    return summed.reshape(frames, pixels, chans).astype(jnp.bfloat16)


def temporal_mix(padded, temporal_weight, frames):
    chans = padded.shape[-1]
    pixels = padded.shape[1]
    total = jnp.zeros((frames * pixels, chans), jnp.float32)
    for tap in range(3):
        total = total + jnp.dot(
            padded[tap : tap + frames].reshape(-1, chans),
            temporal_weight[tap],
            preferred_element_type=jnp.float32,
        )
    return total.reshape(frames, pixels, chans)


def local(
    latent,
    gain_one,
    spatial_weight,
    gain_two,
    temporal_weight,
    gain_three,
    query_weight,
    key_weight,
    value_weight,
    out_weight,
):
    frames_here, rows_here, width, chans = latent.shape
    source = latent.astype(jnp.float32)
    act_one = jax.nn.silu(rms_norm(source, gain_one)).astype(jnp.bfloat16)
    rimmed = extended(act_one, (("row", 1),), 1)
    spatial = lax.conv_general_dilated(
        rimmed,
        spatial_weight,
        (1, 1),
        ((0, 0), (1, 1)),
        dimension_numbers=("NHWC", "HWIO", "NHWC"),
        preferred_element_type=jnp.float32,
    )
    hidden_one = source + spatial
    pixels = rows_here * width
    hidden_flat = hidden_one.reshape(frames_here, pixels, chans)
    act_two = jax.nn.silu(rms_norm(hidden_flat, gain_two)).astype(jnp.bfloat16)
    padded = extended(act_two, (("frame", 0),), 1)
    temporal = temporal_mix(padded, temporal_weight, frames_here)
    hidden_two = hidden_flat + temporal
    normed = rms_norm(hidden_two, gain_three).astype(jnp.bfloat16)
    groups = lax.axis_size("frame")
    per_group = pixels // groups
    moved = lax.all_to_all(
        normed.reshape(frames_here, groups, per_group, chans),
        "frame",
        split_axis=1,
        concat_axis=0,
        tiled=True,
    )
    moved = moved.reshape(frames_here * groups, per_group, chans)
    attended = attend_heads(
        project(moved, query_weight), project(moved, key_weight), project(moved, value_weight)
    ).reshape(frames_here * groups, 1, per_group, chans)
    returned = lax.all_to_all(attended, "frame", split_axis=0, concat_axis=1, tiled=True)
    mixed = jnp.dot(returned.reshape(-1, chans), out_weight, preferred_element_type=jnp.float32)
    result = hidden_two.reshape(-1, chans) + mixed
    return result.reshape(frames_here, rows_here, width, chans)


def solution(mesh):
    return jax.shard_map(
        local,
        mesh=mesh,
        in_specs=(P("frame", "row", None, None), P(), P(), P(), P(), P(), P(), P(), P(), P()),
        out_specs=P("frame", "row", None, None),
        check_vma=False,
    )
```

profile of v0, /device:TPU:63, one launch (start us, length us, event | category | flops | bytes accessed | tf_op | source)
XLA Modules:
  0.0 391.0 jit_solution(15593227416273346015)
XLA Ops:
  0.0 2.7 copy.70
  2.7 1.8 fusion.8
  4.5 2.3 fusion.15
  8.9 2.2 copy.72
  11.2 1.9 collective-permute-start.1
  14.2 3.5 collective-permute-start
  17.7 11.6 %collective-permute-done.1 = bf16[4,1,240,320]{2,3,1,0:T(8,128)(2,1)} collective-permute-done((bf16[4,1,240,320]{2,3,1,0:T(8,128)(2,1)}, bf16[4,1,240,320]{2,3,1,0:T(8,128)(2,1)}, u32[]{:S(2)}, u32[]{:S(2)}) %collective-permute-start.1) | collective-permute-done | bytes 614432 | tf_op jit(solution)/shard_map/ppermute | solution.py:19
  30.8 15.3 %collective-permute-done = bf16[4,1,240,320]{2,3,1,0:T(8,128)(2,1)} collective-permute-done((bf16[4,1,240,320]{2,3,1,0:T(8,128)(2,1)}, bf16[4,1,240,320]{2,3,1,0:T(8,128)(2,1)}, u32[]{:S(2)}, u32[]{:S(2)}) %collective-permute-start) | collective-permute-done | bytes 614432 | tf_op jit(solution)/shard_map/ppermute | solution.py:17
  46.1 2.2 copy.73
  48.3 2.2 maximum_bitcast_fusion
  50.5 2.9 pad
  53.4 5.8 %reshape.119 = bf16[4,4,8,31,320]{4,3,2,1,0:T(8,128)(2,1)} reshape(bf16[4,4,248,320]{3,2,1,0:T(8,128)(2,1)} %pad) | data formatting | bytes 5079040 | tf_op jit(solution)/shard_map/conv_general_dilated | solution.py:84
  60.4 2.4 fusion.4
  62.8 6.6 %fusion.25 = f32[2,32,31,320]{3,1,2,0:T(8,128)S(1)} fusion(bf16[3,3,320,320]{3,2,1,0:T(8,128)(2,1)S(1)} %copy-done, bf16[4,4,8,33,320]{4,3,2,1,0:T(8,128)(2,1)S(1)} %fusion.4, pred[32,31]{0,1:T(8,128)(4,1)S(1)} %copy-done.15), kind=kOutput, calls=%fused_computation.42 | convolution fusion | flops 3657543680 | bytes 7087072 | tf_op jit(solution)/shard_map/conv_general_dilated | solution.py:84
  69.4 3.4 copy.76
  72.8 4.2 %reshape.123 = f32[2,4,248,320]{3,2,1,0:T(8,128)} reshape(f32[2,32,31,320]{3,2,1,0:T(8,128)} %copy.76) | data formatting | bytes 5079040 | tf_op jit(solution)/shard_map/conv_general_dilated | solution.py:84
  77.0 2.8 multiply_reduce_fusion.2
  79.7 3.5 copy.78
  83.2 2.8 copy.83
  86.1 2.0 multiply_convert_fusion
  88.1 4.9 %copy.81 = bf16[4,2,240,320]{2,1,0,3:T(2,128)(2,1)} copy(bf16[4,2,240,320]{3,2,0,1:T(8,128)(2,1)} %multiply_convert_fusion) | data formatting | bytes 2457600 | tf_op jit(solution)/shard_map/convert_element_type | solution.py:95
  93.0 4.9 %convert_element_type.48 = bf16[1920,320]{0,1:T(8,128)(2,1)} reshape(bf16[4,2,240,320]{2,1,0,3:T(2,128)(2,1)} %copy.81) | data formatting | bytes 2457600 | tf_op jit(solution)/shard_map/convert_element_type | solution.py:95
  97.9 4.8 %reshape.109 = f32[4,480,320]{1,2,0:T(8,128)} reshape(f32[4,2,240,320]{2,1,3,0:T(2,128)} %copy.78) | data formatting | bytes 4915200 | tf_op jit(solution)/shard_map/reshape | solution.py:94
  102.7 2.7 multiply_convert_fusion.1
  105.5 3.4 collective-permute-start.3
  108.9 8.1 %collective-permute-start.2 = (bf16[1,480,320]{1,2,0:T(8,128)(2,1)S(1)}, bf16[1,480,320]{1,2,0:T(8,128)(2,1)S(1)}, u32[]{:S(2)}, u32[]{:S(2)}) collective-permute-start(bf16[1,480,320]{1,2,0:T(8,128)(2,1)S(1)} %get-tuple-element.12), channel_id=1, source_target_pairs={{0,16},{16,32},{32,48},{48,64},{64,80},{80,96},{96,112},{112,128},... | collective-permute-start | bytes 921608 | tf_op jit(solution)/shard_map/ppermute | solution.py:17
  117.1 3.3 fusion.29
  120.3 3.1 collective-permute-done.3
  125.9 2.1 copy.82
  128.0 4.3 %reshape.111 = bf16[1920,320]{0,1:T(8,128)(2,1)} reshape(bf16[4,480,320]{1,0,2:T(4,128)(2,1)} %copy.82) | data formatting | bytes 2457600 | tf_op jit(solution)/shard_map/reshape | solution.py:61
  132.3 3.4 copy.80
  135.7 4.0 %reshape.110 = bf16[1920,320]{0,1:T(8,128)(2,1)} reshape(bf16[4,480,320]{1,0,2:T(4,128)(2,1)} %copy.80) | data formatting | bytes 2457600 | tf_op jit(solution)/shard_map/reshape | solution.py:61
  139.7 3.2 convolution_add_fusion.2
  142.9 3.3 convolution_add_fusion.1
  146.2 6.7 %reshape.114 = f32[4,2,240,320]{2,1,0,3:T(2,128)} reshape(f32[1920,320]{0,1:T(8,128)} %convolution_add_fusion.1) | data formatting | bytes 4915200 | tf_op jit(solution)/shard_map/reshape | solution.py:65
  152.9 3.4 copy.84
  156.3 5.6 %copy.86 = f32[4,2,240,320]{3,2,0,1:T(8,128)} copy(f32[4,2,240,320]{2,1,0,3:T(2,128)} %reshape.114) | data formatting | bytes 4915200 | tf_op jit(solution)/shard_map/reshape | solution.py:65
  161.8 2.2 multiply_reduce_fusion.1
  164.4 4.1 %reshape.113 = f32[4,16,30,320]{3,2,1,0:T(8,128)} reshape(f32[1920,320]{1,0:T(8,128)} %copy.84) | data formatting | bytes 4915200 | tf_op jit(solution)/shard_map/reshape | solution.py:65
  168.5 5.0 %fusion.18 = bf16[4,16,30,320]{3,0,2,1:T(4,128)(2,1)S(1)} fusion(f32[4,16,30,320]{3,0,2,1:T(4,128)} %bitcast.76, f32[4,16,30,320]{3,2,1,0:T(8,128)} %reshape.113, f32[320]{0:T(512)S(1)} %copy-done.14, f32[4,16,30]{0,2,1:T(8,128)S(1)} %copy.88), kind=kLoop, calls=%fused_computation.28 | loop fusion | flops 2457600 | bytes 6152960 | tf_op jit(solution)/shard_map/convert_element_type | solution.py:99
  173.5 48.7 %all_to_all.30 = bf16[4,16,30,320]{3,0,2,1:T(4,128)(2,1)S(1)} all-to-all(bf16[4,16,30,320]{3,0,2,1:T(4,128)(2,1)S(1)} %fusion.18), channel_id=1, replica_groups=mesh['frame'=16,'row'=16] {'frame'}, dimensions={1} | all-to-all | bytes 2457600 | tf_op jit(solution)/shard_map/all_to_all | solution.py:102
  223.7 3.6 reshape_reshape.14
  227.3 3.5 convolution_convert_fusion
  230.7 1.9 convolution_convert_fusion.1
  232.7 1.9 convolution_convert_fusion.2
  234.6 15.4 %reshape.127 = bf16[64,30,5,64]{1,0,3,2:T(8,128)(2,1)} reshape(bf16[1920,320]{0,1:T(8,128)(2,1)} %convolution_convert_fusion.2) | data formatting | bytes 2457600 | tf_op jit(solution)/shard_map/reshape;reshape | solution.py:42
  250.0 7.3 %copy.95 = bf16[64,30,5,64]{0,3,2,1:T(8,128)(2,1)} copy(bf16[64,30,5,64]{1,0,3,2:T(8,128)(2,1)} %reshape.127) | data formatting | bytes 2457600 | tf_op jit(solution)/shard_map/reshape;reshape | solution.py:42
  257.3 15.4 %reshape.128 = bf16[64,30,5,64]{1,0,3,2:T(8,128)(2,1)} reshape(bf16[1920,320]{0,1:T(8,128)(2,1)} %convolution_convert_fusion.1) | data formatting | bytes 2457600 | tf_op jit(solution)/shard_map/reshape;reshape | solution.py:40
  272.7 9.9 %copy.93 = bf16[64,30,5,64]{3,0,2,1:T(8,128)(2,1)} copy(bf16[64,30,5,64]{1,0,3,2:T(8,128)(2,1)} %reshape.128) | data formatting | bytes 2457600 | tf_op jit(solution)/shard_map/reshape;reshape | solution.py:40
  282.6 15.6 %reshape.129 = bf16[64,30,5,64]{1,0,3,2:T(8,128)(2,1)} reshape(bf16[1920,320]{0,1:T(8,128)(2,1)} %convolution_convert_fusion) | data formatting | bytes 2457600 | tf_op jit(solution)/shard_map/reshape;reshape | solution.py:41
  298.2 10.0 %copy.94 = bf16[64,30,5,64]{3,0,2,1:T(8,128)(2,1)} copy(bf16[64,30,5,64]{1,0,3,2:T(8,128)(2,1)} %reshape.129) | data formatting | bytes 2457600 | tf_op jit(solution)/shard_map/reshape;reshape | solution.py:41
  308.2 3.9 multiply_reduce_fusion
  313.8 2.7 fusion.1
  316.5 4.7 %copy.97 = bf16[64,1,30,320]{3,2,1,0:T(8,128)(2,1)} copy(bf16[64,1,30,320]{0,3,2,1:T(8,128)(2,1)} %bitcast.79) | data formatting | bytes 2457600 | tf_op jit(solution)/shard_map/convert_element_type | solution.py:52
  321.2 6.4 %all-to-all-start.1 = ((bf16[64,1,30,320]{3,2,1,0:T(8,128)(2,1)}), bf16[64,1,30,320]{3,2,1,0:T(8,128)(2,1)}, u32[]{:S(2)}, u32[]{:S(2)}) async-start(bf16[64,1,30,320]{3,2,1,0:T(8,128)(2,1)} %copy.97), calls=%async_computation.1 | async-start | bytes 3145728 | tf_op jit(solution)/shard_map/all_to_all | solution.py:113
  327.6 3.3 copy.77
  330.9 5.0 %reshape.108 = f32[1920,320]{0,1:T(8,128)} reshape(f32[4,2,240,320]{2,1,0,3:T(2,128)} %copy.77) | data formatting | bytes 4915200 | tf_op jit(solution)/shard_map/reshape | solution.py:94
  335.9 31.6 %all-to-all-done.1 = bf16[64,1,30,320]{3,2,1,0:T(8,128)(2,1)} async-done(((bf16[64,1,30,320]{3,2,1,0:T(8,128)(2,1)}), bf16[64,1,30,320]{3,2,1,0:T(8,128)(2,1)}, u32[]{:S(2)}, u32[]{:S(2)}) %all-to-all-start.1) | async-done | bytes 1228832 | tf_op jit(solution)/shard_map/all_to_all | solution.py:113
  367.6 2.2 copy.123
  369.8 2.0 copy.99
  371.8 3.5 reshape.115
  375.3 4.5 %convolution_add_fusion = f32[1920,320]{0,1:T(8,128)} fusion(bf16[1920,320]{1,0:T(8,128)(2,1)} %reshape.115, bf16[320,320]{1,0:T(8,128)(2,1)S(1)} %copy-done.11, f32[1920,320]{0,1:T(8,128)} %reshape.108, f32[1920,320]{0,1:T(8,128)S(1)} %copy-done.2), kind=kOutput, calls=%fused_computation.32 | convolution fusion | flops 394444800 | bytes 8806400 | tf_op jit(solution)/shard_map/dot_general | solution.py:114
  379.8 6.9 %reshape.116 = f32[4,2,240,320]{2,1,0,3:T(2,128)} reshape(f32[1920,320]{0,1:T(8,128)} %convolution_add_fusion) | data formatting | bytes 4915200 | tf_op jit(solution)/shard_map/reshape | solution.py:116
  386.7 4.1 %copy.100 = f32[4,2,240,320]{2,3,1,0:T(8,128)} copy(f32[4,2,240,320]{2,1,0,3:T(2,128)} %reshape.116) | data formatting | bytes 4915200 | tf_op jit(solution)/shard_map/reshape | solution.py:116
  (49 shorter events, 12.1 us)
Async XLA Ops:
  0.0 62.8 %copy-start = (bf16[3,3,320,320]{3,2,1,0:T(8,128)(2,1)S(1)}, bf16[3,3,320,320]{3,2,1,0:T(8,128)(2,1)}, u32[]{:S(2)}) copy-start(bf16[3,3,320,320]{3,2,1,0:T(8,128)(2,1)} %param.12) | copy-start | bytes 5529604
  0.0 4.5 %copy-start.13 = (f32[320]{0:T(512)S(1)}, f32[320]{0:T(512)}, u32[]{:S(2)}) copy-start(f32[320]{0:T(512)} %param.11) | copy-start | bytes 3844
  6.8 1.1 copy-start.4
  11.2 18.2 %collective-permute-start.1 = (bf16[4,1,240,320]{2,3,1,0:T(8,128)(2,1)}, bf16[4,1,240,320]{2,3,1,0:T(8,128)(2,1)}, u32[]{:S(2)}, u32[]{:S(2)}) collective-permute-start(bf16[4,1,240,320]{2,3,1,0:T(8,128)(2,1)} %copy.72), channel_id=1, source_target_pairs={{1,0},{2,1},{3,2},{4,3},{5,4},{6,5},{7,6},{8,7},{9,8},{10,9},{11,1... | collective-permute-start | bytes 1843208 | tf_op jit(solution)/shard_map/ppermute | solution.py:19
  14.2 31.9 %collective-permute-start = (bf16[4,1,240,320]{2,3,1,0:T(8,128)(2,1)}, bf16[4,1,240,320]{2,3,1,0:T(8,128)(2,1)}, u32[]{:S(2)}, u32[]{:S(2)}) collective-permute-start(bf16[4,1,240,320]{2,3,1,0:T(8,128)(2,1)} %copy.71), channel_id=1, source_target_pairs={{0,1},{1,2},{2,3},{3,4},{4,5},{5,6},{6,7},{7,8},{8,9},{9,10},{10,1... | collective-permute-start | bytes 1843208 | tf_op jit(solution)/shard_map/ppermute | solution.py:17
  60.4 2.4 copy-start.15
  83.2 2.9 copy-start.12
  102.7 14.4 %copy-start.5 = (bf16[1920,320]{0,1:T(8,128)(2,1)S(1)}, bf16[1920,320]{0,1:T(8,128)(2,1)}, u32[]{:S(2)}) copy-start(bf16[1920,320]{0,1:T(8,128)(2,1)} %convert_element_type.48) | copy-start | bytes 3686404
  105.5 17.9 %collective-permute-start.3 = (bf16[1,480,320]{1,2,0:T(8,128)(2,1)S(1)}, bf16[1,480,320]{1,2,0:T(8,128)(2,1)S(1)}, u32[]{:S(2)}, u32[]{:S(2)}) collective-permute-start(bf16[1,480,320]{1,2,0:T(8,128)(2,1)S(1)} %get-tuple-element.11), channel_id=1, source_target_pairs={{16,0},{32,16},{48,32},{64,48},{80,64},{96,80},{112,96},{128,112},... | collective-permute-start | bytes 921608 | tf_op jit(solution)/shard_map/ppermute | solution.py:19
  108.9 15.7 %collective-permute-start.2 = (bf16[1,480,320]{1,2,0:T(8,128)(2,1)S(1)}, bf16[1,480,320]{1,2,0:T(8,128)(2,1)S(1)}, u32[]{:S(2)}, u32[]{:S(2)}) collective-permute-start(bf16[1,480,320]{1,2,0:T(8,128)(2,1)S(1)} %get-tuple-element.12), channel_id=1, source_target_pairs={{0,16},{16,32},{32,48},{48,64},{64,80},{80,96},{96,112},{112,128},... | collective-permute-start | bytes 921608 | tf_op jit(solution)/shard_map/ppermute | solution.py:17
  139.7 3.2 copy-start.6
  164.4 4.1 %copy-start.14 = (f32[320]{0:T(512)S(1)}, f32[320]{0:T(512)}, u32[]{:S(2)}) copy-start(f32[320]{0:T(512)} %param.15) | copy-start | bytes 3844
  222.3 5.0 %copy-start.8 = (bf16[320,320]{1,0:T(8,128)(2,1)S(1)}, bf16[320,320]{1,0:T(8,128)(2,1)}, u32[]{:S(2)}) copy-start(bf16[320,320]{1,0:T(8,128)(2,1)} %param.17) | copy-start | bytes 614404
  223.7 7.0 %copy-start.9 = (bf16[320,320]{1,0:T(8,128)(2,1)S(1)}, bf16[320,320]{1,0:T(8,128)(2,1)}, u32[]{:S(2)}) copy-start(bf16[320,320]{1,0:T(8,128)(2,1)} %param.16) | copy-start | bytes 614404
  227.3 3.5 copy-start.3
  227.3 5.4 %copy-start.10 = (bf16[320,320]{1,0:T(8,128)(2,1)S(1)}, bf16[320,320]{1,0:T(8,128)(2,1)}, u32[]{:S(2)}) copy-start(bf16[320,320]{1,0:T(8,128)(2,1)} %param.18) | copy-start | bytes 614404
  312.1 1.7 copy-start.7
  321.2 46.4 %all-to-all-start.1 = ((bf16[64,1,30,320]{3,2,1,0:T(8,128)(2,1)}), bf16[64,1,30,320]{3,2,1,0:T(8,128)(2,1)}, u32[]{:S(2)}, u32[]{:S(2)}) async-start(bf16[64,1,30,320]{3,2,1,0:T(8,128)(2,1)} %copy.97), calls=%async_computation.1 | async-start | bytes 3145728 | tf_op jit(solution)/shard_map/all_to_all | solution.py:113
  369.7 5.6 %copy-start.2 = (f32[1920,320]{0,1:T(8,128)S(1)}, f32[1920,320]{0,1:T(8,128)}, u32[]{:S(2)}) copy-start(f32[1920,320]{0,1:T(8,128)} %convolution_add_fusion.1) | copy-start | bytes 7372804
  369.7 5.6 %copy-start.11 = (bf16[320,320]{1,0:T(8,128)(2,1)S(1)}, bf16[320,320]{1,0:T(8,128)(2,1)}, u32[]{:S(2)}) copy-start(bf16[320,320]{1,0:T(8,128)(2,1)} %param.19) | copy-start | bytes 614404
  379.8 10.9 %copy-start.1 = (bf16[3,3,320,320]{3,2,1,0:T(8,128)(2,1)S(1)}, bf16[3,3,320,320]{3,2,1,0:T(8,128)(2,1)}, u32[]{:S(2)}) copy-start(bf16[3,3,320,320]{3,2,1,0:T(8,128)(2,1)} %param.12) | copy-start | bytes 5529604
where the time goes:
time: 397 us; the launch traced here: 391 us
  local copies, waits for them, and re-layouts  195 us (49%)
  waiting for transfers between devices  62.7 us (16%)
  blocking collectives  48.7 us (12%)
  matrix products  34.7 us (9%)
  other arithmetic  26.2 us (7%)
  starting transfers between devices  23.4 us (6%)
    all_to_all x1, blocking collectives, local(): lax.all_to_all(normed.reshape(frames_here, groups, per_group, chans), 'fr...  48.7 us
    all_to_all x1, waiting for transfers between devices, local(): lax.all_to_all(attended, 'frame', split_axis=0, concat_axis=1, tiled=True)  31.6 us
    another operation x2, local copies, waits for them, and re-layouts, attend_heads(): k_split = keys.reshape(frames, pixels, heads, HEAD_DIM)  25.6 us
    another operation x2, local copies, waits for them, and re-layouts, attend_heads(): q_split = queries.reshape(frames, pixels, heads, HEAD_DIM)  25.3 us
    another operation x2, local copies, waits for them, and re-layouts, attend_heads(): v_split = values.reshape(frames, pixels, heads, HEAD_DIM)  22.7 us
    ppermute x2, waiting for transfers between devices, extended(): lax.ppermute(tail, axis, [(i, (i + 1) % count) for i in range(ends)])  16.5 us
    reshape x3, local copies, waits for them, and re-layouts, temporal_mix(): return total.reshape(frames, pixels, chans)  16.4 us
    ppermute x2, waiting for transfers between devices, extended(): lax.ppermute(head, axis, [((i + 1) % count, i) for i in range(ends)])  14.6 us
  transfers between devices with their start and end apart: 5, of which 5 were waited for; matrix products, arithmetic and copies ran while one was open for 4% of the time, Pallas kernels for 0%

commit v1 on v0

--- a/solution.py
+++ b/solution.py
@@ -1,9 +1,22 @@
+import functools
 import jax
 import jax.numpy as jnp
 from jax import lax
 from jax.sharding import PartitionSpec as P
 
 HEAD_DIM = 64
+
+
+def work_ends(mine_x, out_dim, pos_dim):
+    part_next = lax.axis_size("frame")
+    t1 = jnp.split(mine_x, part_next, axis=out_dim)
+    formed = jnp.stack(t1, axis=0)
+    before = lax.all_to_all(formed, axis_name="frame", split_axis=0, concat_axis=0)
+    r1 = jnp.concatenate(before, axis=pos_dim)
+    return r1
+
+
+post_field = functools.partial(work_ends, out_dim=0, pos_dim=1)
 
 
 def extended(cells, sides, width):
@@ -110,7 +123,7 @@
     attended = attend_heads(
         project(moved, query_weight), project(moved, key_weight), project(moved, value_weight)
     ).reshape(frames_here * groups, 1, per_group, chans)
-    returned = lax.all_to_all(attended, "frame", split_axis=0, concat_axis=1, tiled=True)
+    returned = post_field(attended)
     mixed = jnp.dot(returned.reshape(-1, chans), out_weight, preferred_element_type=jnp.float32)
     result = hidden_two.reshape(-1, chans) + mixed
     return result.reshape(frames_here, rows_here, width, chans)

time: 397 us -> 441 us (1.11)
  local copies, waits for them, and re-layouts: 195 us -> 242 us
    unnamed x33 -> x56, local copies, waits for them, and re-layouts: 4.05 us -> 25.6 us
    another operation x0 -> x18, local copies, waits for them, and re-layouts: none -> 17.4 us  [the longest x17 13.9 us: work_ends(): formed = jnp.stack(t1, axis=0)]
    split x0 -> x17, local copies, waits for them, and re-layouts: none -> 14.6 us  [work_ends(): t1 = jnp.split(mine_x, part_next, axis=out_dim)]
    convert_element_type x1 -> x0, local copies, waits for them, and re-layouts: 4.71 us -> none  [attend_heads(): return summed.reshape(frames, pixels, chans).astype(jnp.bfloat16)]
  transfers between devices with their start and end apart: 5 -> 5, of which waited for: 5 -> 5; matrix products, arithmetic and copies ran while one was open for 4% -> 3% of each run, Pallas kernels for 0% -> 0%
where the time goes in v1:
time: 441 us; the launch traced here: 435 us
  local copies, waits for them, and re-layouts  242 us (55%)
  waiting for transfers between devices  60.4 us (14%)
  blocking collectives  48.7 us (11%)
  matrix products  34.8 us (8%)
  other arithmetic  24.9 us (6%)
  starting transfers between devices  23.4 us (5%)
    all_to_all x1, blocking collectives, local(): lax.all_to_all(normed.reshape(frames_here, groups, per_group, chans), 'fr...  48.7 us
    all_to_all x1, waiting for transfers between devices, work_ends(): lax.all_to_all(formed, axis_name='frame', split_axis=0, concat_axis=0)  29.3 us
    unnamed x56, local copies, waits for them, and re-layouts  25.6 us
    another operation x2, local copies, waits for them, and re-layouts, attend_heads(): k_split = keys.reshape(frames, pixels, heads, HEAD_DIM)  25.6 us
    another operation x2, local copies, waits for them, and re-layouts, attend_heads(): v_split = values.reshape(frames, pixels, heads, HEAD_DIM)  25.4 us
    another operation x2, local copies, waits for them, and re-layouts, attend_heads(): q_split = queries.reshape(frames, pixels, heads, HEAD_DIM)  25.3 us
    ppermute x2, waiting for transfers between devices, extended(): lax.ppermute(tail, axis, [(i, (i + 1) % count) for i in range(ends)])  16.5 us
    reshape x3, local copies, waits for them, and re-layouts, temporal_mix(): return total.reshape(frames, pixels, chans)  16.4 us
  transfers between devices with their start and end apart: 5, of which 5 were waited for; matrix products, arithmetic and copies ran while one was open for 3% of the time, Pallas kernels for 0%

profile of v1, /device:TPU:63, one launch (start us, length us, event | category | flops | bytes accessed | tf_op | source)
XLA Modules:
  0.0 434.5 jit_solution(2943173376235627700)
XLA Ops:
  0.0 2.7 copy.100
  2.7 1.9 fusion.8
  7.7 2.3 copy.102
  9.9 1.9 collective-permute-start.1
  13.0 3.5 collective-permute-start
  16.5 11.6 %collective-permute-done.1 = bf16[4,1,240,320]{2,3,1,0:T(8,128)(2,1)} collective-permute-done((bf16[4,1,240,320]{2,3,1,0:T(8,128)(2,1)}, bf16[4,1,240,320]{2,3,1,0:T(8,128)(2,1)}, u32[]{:S(2)}, u32[]{:S(2)}) %collective-permute-start.1) | collective-permute-done | bytes 614432 | tf_op jit(solution)/shard_map/ppermute | solution.py:32
  29.6 15.3 %collective-permute-done = bf16[4,1,240,320]{2,3,1,0:T(8,128)(2,1)} collective-permute-done((bf16[4,1,240,320]{2,3,1,0:T(8,128)(2,1)}, bf16[4,1,240,320]{2,3,1,0:T(8,128)(2,1)}, u32[]{:S(2)}, u32[]{:S(2)}) %collective-permute-start) | collective-permute-done | bytes 614432 | tf_op jit(solution)/shard_map/ppermute | solution.py:30
  44.9 2.2 copy.103
  47.1 2.2 maximum_bitcast_fusion
  49.3 2.9 pad
  52.2 5.8 %reshape.172 = bf16[4,4,8,31,320]{4,3,2,1,0:T(8,128)(2,1)} reshape(bf16[4,4,248,320]{3,2,1,0:T(8,128)(2,1)} %pad) | data formatting | bytes 5079040 | tf_op jit(solution)/shard_map/conv_general_dilated | solution.py:97
  59.2 2.4 fusion.4
  61.6 6.6 %fusion.25 = f32[2,32,31,320]{3,1,2,0:T(8,128)S(1)} fusion(bf16[3,3,320,320]{3,2,1,0:T(8,128)(2,1)S(1)} %copy-done, bf16[4,4,8,33,320]{4,3,2,1,0:T(8,128)(2,1)S(1)} %fusion.4, pred[32,31]{0,1:T(8,128)(4,1)S(1)} %copy-done.19), kind=kOutput, calls=%fused_computation.42 | convolution fusion | flops 3657543680 | bytes 7087072 | tf_op jit(solution)/shard_map/conv_general_dilated | solution.py:97
  68.2 3.4 copy.106
  71.6 4.2 reshape.176
  75.8 2.8 multiply_reduce_fusion.2
  78.5 3.5 copy.108
  82.0 2.8 copy.113
  84.9 2.0 multiply_convert_fusion
  86.9 4.9 %copy.111 = bf16[4,2,240,320]{2,1,0,3:T(2,128)(2,1)} copy(bf16[4,2,240,320]{3,2,0,1:T(8,128)(2,1)} %multiply_convert_fusion) | data formatting | bytes 2457600 | tf_op jit(solution)/shard_map/convert_element_type | solution.py:108
  91.8 4.9 %convert_element_type.39 = bf16[1920,320]{0,1:T(8,128)(2,1)} reshape(bf16[4,2,240,320]{2,1,0,3:T(2,128)(2,1)} %copy.111) | data formatting | bytes 2457600 | tf_op jit(solution)/shard_map/convert_element_type | solution.py:108
  96.7 4.8 %reshape.162 = f32[4,480,320]{1,2,0:T(8,128)} reshape(f32[4,2,240,320]{2,1,3,0:T(2,128)} %copy.108) | data formatting | bytes 4915200 | tf_op jit(solution)/shard_map/reshape | solution.py:107
  101.5 2.7 multiply_convert_fusion.1
  104.3 3.4 collective-permute-start.3
  107.8 8.1 %collective-permute-start.2 = (bf16[1,480,320]{1,2,0:T(8,128)(2,1)S(1)}, bf16[1,480,320]{1,2,0:T(8,128)(2,1)S(1)}, u32[]{:S(2)}, u32[]{:S(2)}) collective-permute-start(bf16[1,480,320]{1,2,0:T(8,128)(2,1)S(1)} %get-tuple-element.28), channel_id=1, source_target_pairs={{0,16},{16,32},{32,48},{48,64},{64,80},{80,96},{96,112},{112,128},... | collective-permute-start | bytes 921608 | tf_op jit(solution)/shard_map/ppermute | solution.py:30
  115.9 3.3 fusion.29
  119.2 3.1 collective-permute-done.3
  124.8 2.1 copy.112
  126.8 4.4 %reshape.164 = bf16[1920,320]{0,1:T(8,128)(2,1)} reshape(bf16[4,480,320]{1,0,2:T(4,128)(2,1)} %copy.112) | data formatting | bytes 2457600 | tf_op jit(solution)/shard_map/reshape | solution.py:74
  131.2 3.4 copy.110
  134.6 4.0 reshape.163
  138.6 3.2 convolution_add_fusion.2
  141.8 3.3 convolution_add_fusion.1
  145.1 6.7 %reshape.167 = f32[4,2,240,320]{2,1,0,3:T(2,128)} reshape(f32[1920,320]{0,1:T(8,128)} %convolution_add_fusion.1) | data formatting | bytes 4915200 | tf_op jit(solution)/shard_map/reshape | solution.py:78
  151.8 3.4 copy.114
  155.2 5.6 %copy.116 = f32[4,2,240,320]{3,2,0,1:T(8,128)} copy(f32[4,2,240,320]{2,1,0,3:T(2,128)} %reshape.167) | data formatting | bytes 4915200 | tf_op jit(solution)/shard_map/reshape | solution.py:78
  160.8 2.2 multiply_reduce_fusion.1
  163.3 4.1 reshape.166
  167.5 5.0 %fusion.18 = bf16[4,16,30,320]{3,0,2,1:T(4,128)(2,1)S(1)} fusion(f32[4,16,30,320]{3,0,2,1:T(4,128)} %bitcast.104, f32[4,16,30,320]{3,2,1,0:T(8,128)} %reshape.166, f32[320]{0:T(512)S(1)} %copy-done.18, f32[4,16,30]{0,2,1:T(8,128)S(1)} %copy.118), kind=kLoop, calls=%fused_computation.28 | loop fusion | flops 2457600 | bytes 6152960 | tf_op jit(solution)/shard_map/convert_element_type | solution.py:112
  172.5 48.7 %all_to_all.20 = bf16[4,16,30,320]{3,0,2,1:T(4,128)(2,1)S(1)} all-to-all(bf16[4,16,30,320]{3,0,2,1:T(4,128)(2,1)S(1)} %fusion.18), channel_id=1, replica_groups=mesh['frame'=16,'row'=16] {'frame'}, dimensions={1} | all-to-all | bytes 2457600 | tf_op jit(solution)/shard_map/all_to_all | solution.py:115
  222.7 3.6 reshape_reshape.17
  226.2 3.4 convolution_convert_fusion
  229.7 1.9 convolution_convert_fusion.1
  231.6 1.9 convolution_convert_fusion.2
  233.5 15.4 %reshape.180 = bf16[64,30,5,64]{1,0,3,2:T(8,128)(2,1)} reshape(bf16[1920,320]{0,1:T(8,128)(2,1)} %convolution_convert_fusion.2) | data formatting | bytes 2457600 | tf_op jit(solution)/shard_map/reshape;reshape | solution.py:55
  248.9 10.0 %copy.125 = bf16[64,30,5,64]{3,0,2,1:T(8,128)(2,1)} copy(bf16[64,30,5,64]{1,0,3,2:T(8,128)(2,1)} %reshape.180) | data formatting | bytes 2457600 | tf_op jit(solution)/shard_map/reshape;reshape | solution.py:55
  258.9 15.4 %reshape.181 = bf16[64,30,5,64]{1,0,3,2:T(8,128)(2,1)} reshape(bf16[1920,320]{0,1:T(8,128)(2,1)} %convolution_convert_fusion.1) | data formatting | bytes 2457600 | tf_op jit(solution)/shard_map/reshape;reshape | solution.py:53
  274.3 9.9 %copy.123 = bf16[64,30,5,64]{3,0,2,1:T(8,128)(2,1)} copy(bf16[64,30,5,64]{1,0,3,2:T(8,128)(2,1)} %reshape.181) | data formatting | bytes 2457600 | tf_op jit(solution)/shard_map/reshape;reshape | solution.py:53
  284.3 15.6 %reshape.182 = bf16[64,30,5,64]{1,0,3,2:T(8,128)(2,1)} reshape(bf16[1920,320]{0,1:T(8,128)(2,1)} %convolution_convert_fusion) | data formatting | bytes 2457600 | tf_op jit(solution)/shard_map/reshape;reshape | solution.py:54
  299.9 10.0 %copy.124 = bf16[64,30,5,64]{3,0,2,1:T(8,128)(2,1)} copy(bf16[64,30,5,64]{1,0,3,2:T(8,128)(2,1)} %reshape.182) | data formatting | bytes 2457600 | tf_op jit(solution)/shard_map/reshape;reshape | solution.py:54
  309.9 3.9 multiply_reduce_fusion
  315.4 2.8 fusion.1
  318.2 1.9 fusion.36
  349.2 1.6 constant_dynamic-update-slice_fusion.13
  361.7 1.6 constant_dynamic-update-slice_fusion.5
  368.4 6.4 %all-to-all-start.1 = ((bf16[16,4,1,30,320]{4,1,3,2,0:T(4,128)(2,1)}), bf16[16,4,1,30,320]{4,1,3,2,0:T(4,128)(2,1)}, u32[]{:S(2)}, u32[]{:S(2)}) async-start(bf16[16,4,1,30,320]{4,1,3,2,0:T(4,128)(2,1)} %constant_dynamic-update-slice_fusion), calls=%async_computation.1 | async-start | bytes 2949120 | tf_op jit(solution)/shard_map/all_to_all | solution.py:14
  374.8 3.3 copy.107
  378.1 5.0 %reshape.161 = f32[1920,320]{0,1:T(8,128)} reshape(f32[4,2,240,320]{2,1,0,3:T(2,128)} %copy.107) | data formatting | bytes 4915200 | tf_op jit(solution)/shard_map/reshape | solution.py:107
  383.1 29.3 %all-to-all-done.1 = bf16[16,4,1,30,320]{4,1,3,2,0:T(4,128)(2,1)} async-done(((bf16[16,4,1,30,320]{4,1,3,2,0:T(4,128)(2,1)}), bf16[16,4,1,30,320]{4,1,3,2,0:T(4,128)(2,1)}, u32[]{:S(2)}, u32[]{:S(2)}) %all-to-all-start.1) | async-done | bytes 1228832 | tf_op jit(solution)/shard_map/all_to_all | solution.py:14
  412.4 2.9 copy.143
  415.3 3.5 reshape_reshape.21
  418.8 4.5 %convolution_add_fusion = f32[1920,320]{0,1:T(8,128)} fusion(bf16[1920,320]{1,0:T(8,128)(2,1)} %reshape_reshape.21, bf16[320,320]{1,0:T(8,128)(2,1)S(1)} %copy-done.15, f32[1920,320]{0,1:T(8,128)} %reshape.161, f32[1920,320]{0,1:T(8,128)S(1)} %copy-done.2), kind=kOutput, calls=%fused_computation.32 | convolution fusion | flops 394444800 | bytes 8806400 | tf_op jit(solution)/shard_map/dot_general | solution.py:127
  423.3 6.9 %reshape.169 = f32[4,2,240,320]{2,1,0,3:T(2,128)} reshape(f32[1920,320]{0,1:T(8,128)} %convolution_add_fusion) | data formatting | bytes 4915200 | tf_op jit(solution)/shard_map/reshape | solution.py:129
  430.1 4.1 copy.144
  (104 shorter events, 57.9 us)
Async XLA Ops:
  0.0 61.6 %copy-start = (bf16[3,3,320,320]{3,2,1,0:T(8,128)(2,1)S(1)}, bf16[3,3,320,320]{3,2,1,0:T(8,128)(2,1)}, u32[]{:S(2)}) copy-start(bf16[3,3,320,320]{3,2,1,0:T(8,128)(2,1)} %param.12) | copy-start | bytes 5529604
  0.0 4.6 %copy-start.17 = (f32[320]{0:T(512)S(1)}, f32[320]{0:T(512)}, u32[]{:S(2)}) copy-start(f32[320]{0:T(512)} %param.11) | copy-start | bytes 3844
  2.7 1.9 copy-start.3
  5.5 1.1 copy-start.5
  9.9 18.2 %collective-permute-start.1 = (bf16[4,1,240,320]{2,3,1,0:T(8,128)(2,1)}, bf16[4,1,240,320]{2,3,1,0:T(8,128)(2,1)}, u32[]{:S(2)}, u32[]{:S(2)}) collective-permute-start(bf16[4,1,240,320]{2,3,1,0:T(8,128)(2,1)} %copy.102), channel_id=1, source_target_pairs={{1,0},{2,1},{3,2},{4,3},{5,4},{6,5},{7,6},{8,7},{9,8},{10,9},{11,1... | collective-permute-start | bytes 1843208 | tf_op jit(solution)/shard_map/ppermute | solution.py:32
  13.0 31.9 %collective-permute-start = (bf16[4,1,240,320]{2,3,1,0:T(8,128)(2,1)}, bf16[4,1,240,320]{2,3,1,0:T(8,128)(2,1)}, u32[]{:S(2)}, u32[]{:S(2)}) collective-permute-start(bf16[4,1,240,320]{2,3,1,0:T(8,128)(2,1)} %copy.101), channel_id=1, source_target_pairs={{0,1},{1,2},{2,3},{3,4},{4,5},{5,6},{6,7},{7,8},{8,9},{9,10},{10,1... | collective-permute-start | bytes 1843208 | tf_op jit(solution)/shard_map/ppermute | solution.py:30
  59.2 2.4 copy-start.19
  82.0 2.9 copy-start.16
  101.5 14.4 %copy-start.6 = (bf16[1920,320]{0,1:T(8,128)(2,1)S(1)}, bf16[1920,320]{0,1:T(8,128)(2,1)}, u32[]{:S(2)}) copy-start(bf16[1920,320]{0,1:T(8,128)(2,1)} %convert_element_type.39) | copy-start | bytes 3686404
  104.3 17.9 %collective-permute-start.3 = (bf16[1,480,320]{1,2,0:T(8,128)(2,1)S(1)}, bf16[1,480,320]{1,2,0:T(8,128)(2,1)S(1)}, u32[]{:S(2)}, u32[]{:S(2)}) collective-permute-start(bf16[1,480,320]{1,2,0:T(8,128)(2,1)S(1)} %get-tuple-element.27), channel_id=1, source_target_pairs={{16,0},{32,16},{48,32},{64,48},{80,64},{96,80},{112,96},{128,112},... | collective-permute-start | bytes 921608 | tf_op jit(solution)/shard_map/ppermute | solution.py:32
  107.8 15.7 %collective-permute-start.2 = (bf16[1,480,320]{1,2,0:T(8,128)(2,1)S(1)}, bf16[1,480,320]{1,2,0:T(8,128)(2,1)S(1)}, u32[]{:S(2)}, u32[]{:S(2)}) collective-permute-start(bf16[1,480,320]{1,2,0:T(8,128)(2,1)S(1)} %get-tuple-element.28), channel_id=1, source_target_pairs={{0,16},{16,32},{32,48},{48,64},{64,80},{80,96},{96,112},{112,128},... | collective-permute-start | bytes 921608 | tf_op jit(solution)/shard_map/ppermute | solution.py:30
  138.6 3.2 copy-start.7
  163.3 4.1 copy-start.18
  221.2 5.0 %copy-start.12 = (bf16[320,320]{1,0:T(8,128)(2,1)S(1)}, bf16[320,320]{1,0:T(8,128)(2,1)}, u32[]{:S(2)}) copy-start(bf16[320,320]{1,0:T(8,128)(2,1)} %param.17) | copy-start | bytes 614404
  222.7 7.0 %copy-start.13 = (bf16[320,320]{1,0:T(8,128)(2,1)S(1)}, bf16[320,320]{1,0:T(8,128)(2,1)}, u32[]{:S(2)}) copy-start(bf16[320,320]{1,0:T(8,128)(2,1)} %param.16) | copy-start | bytes 614404
  226.2 3.4 copy-start.4
  226.2 5.4 %copy-start.14 = (bf16[320,320]{1,0:T(8,128)(2,1)S(1)}, bf16[320,320]{1,0:T(8,128)(2,1)}, u32[]{:S(2)}) copy-start(bf16[320,320]{1,0:T(8,128)(2,1)} %param.18) | copy-start | bytes 614404
  313.7 1.7 copy-start.8
  344.4 22.6 %copy-start.10 = (bf16[1,4,1,30,320]{4,1,3,2,0:T(4,128)(2,1)S(1)}, bf16[1,4,1,30,320]{4,1,3,2,0:T(4,128)(2,1)}, u32[]{:S(2)}) copy-start(bf16[1,4,1,30,320]{4,1,3,2,0:T(4,128)(2,1)} %stack.65) | copy-start | bytes 230404
  344.4 23.3 %copy-start.9 = (bf16[1,4,1,30,320]{4,1,3,2,0:T(4,128)(2,1)S(1)}, bf16[1,4,1,30,320]{4,1,3,2,0:T(4,128)(2,1)}, u32[]{:S(2)}) copy-start(bf16[1,4,1,30,320]{4,1,3,2,0:T(4,128)(2,1)} %stack.66) | copy-start | bytes 230404
  345.3 21.1 %copy-start.11 = (bf16[1,4,1,30,320]{4,1,3,2,0:T(4,128)(2,1)S(1)}, bf16[1,4,1,30,320]{4,1,3,2,0:T(4,128)(2,1)}, u32[]{:S(2)}) copy-start(bf16[1,4,1,30,320]{4,1,3,2,0:T(4,128)(2,1)} %stack.64) | copy-start | bytes 230404
  368.4 44.0 %all-to-all-start.1 = ((bf16[16,4,1,30,320]{4,1,3,2,0:T(4,128)(2,1)}), bf16[16,4,1,30,320]{4,1,3,2,0:T(4,128)(2,1)}, u32[]{:S(2)}, u32[]{:S(2)}) async-start(bf16[16,4,1,30,320]{4,1,3,2,0:T(4,128)(2,1)} %constant_dynamic-update-slice_fusion), calls=%async_computation.1 | async-start | bytes 2949120 | tf_op jit(solution)/shard_map/all_to_all | solution.py:14
  412.4 6.4 %copy-start.2 = (f32[1920,320]{0,1:T(8,128)S(1)}, f32[1920,320]{0,1:T(8,128)}, u32[]{:S(2)}) copy-start(f32[1920,320]{0,1:T(8,128)} %convolution_add_fusion.1) | copy-start | bytes 7372804
  412.4 6.4 %copy-start.15 = (bf16[320,320]{1,0:T(8,128)(2,1)S(1)}, bf16[320,320]{1,0:T(8,128)(2,1)}, u32[]{:S(2)}) copy-start(bf16[320,320]{1,0:T(8,128)(2,1)} %param.19) | copy-start | bytes 614404
  423.3 10.9 %copy-start.1 = (bf16[3,3,320,320]{3,2,1,0:T(8,128)(2,1)S(1)}, bf16[3,3,320,320]{3,2,1,0:T(8,128)(2,1)}, u32[]{:S(2)}) copy-start(bf16[3,3,320,320]{3,2,1,0:T(8,128)(2,1)} %param.12) | copy-start | bytes 5529604
